TPU v7x, 256 devices: a whole 4x4x8 slice. The times are simulated.
256 devices in a mesh: shot: 16 (over x_lo, z), rcv: 8 (over y, x_hi), surf: 2 (over core).
Axes of the slice: x: 4 (x_hi: 2, x_lo: 2; x = x_hi * 2 + x_lo), y: 4, z: 8, core: 2. Of those that a mesh axis runs over, the one named last changes fastest.
Arguments:
- traces: bfloat16 [2, 16384, 256], P('surf', 'shot'), may hold values from -6 to 6
- trace_block: int32 [2, 16384, 1], P('surf', 'shot'), may hold values from 0 to 15; in each aligned block of 128 rows (0 to 127, 128 to 255, ..., all dimensions but the last counted through in order) at most 16 rows name the same one
- trace_shot: int32 [2, 16384], P('surf', 'shot'), may hold values from 0 to 15
- trace_point: int32 [2, 16384], P('surf', 'shot'), may hold values from 0 to 255
- recv_panel: bfloat16 [129, 2, 512, 1024], P(None, None, ('shot', 'surf'), 'rcv'), may hold values from -0.375 to 0.375
Outputs:
- multiples: bfloat16 [129, 2, 256, 1024], P(None, None, ('shot', 'surf'), 'rcv')
Inputs may be any that keep to these rules, and one draw needn't show every extreme that they name: `trace_block`: in each aligned block of 128 rows, at most 16 rows name one shot block.
All inputs are finite; a program needn't handle non-finite values.
Results may differ from a plain program's by a relative error of at most 0.012.
Values may be sent and summed in bfloat16 or wider, within the bound.
A program may use at most 64 MiB of HBM per device.

v0:
```python
import math
import jax
import jax.numpy as jnp
from jax import lax
from jax.sharding import PartitionSpec as P

SHOTS_PER_INDEX = 16


def split_up(array, dim, size):
    before, after = (array.shape[:dim], array.shape[dim + 1 :])
    return jnp.moveaxis(array.reshape(*before, size, -1, *after), dim, 0)


def summed_on_arrival(array, axis, dim):
    size = lax.axis_size(axis)
    parts = lax.all_to_all(split_up(array, dim, size), axis, 0, 0, tiled=True)
    return jnp.sum(parts.astype(jnp.float32), axis=0)


def transform_rows(samples, window_len, bin_count):
    sample_index = lax.broadcasted_iota(jnp.int32, (window_len, bin_count), 0)
    freq_index = lax.broadcasted_iota(jnp.int32, (window_len, bin_count), 1)
    phase_angle = (sample_index * freq_index % window_len).astype(jnp.float32) * (
        2.0 * math.pi / window_len
    )
    norm_factor = 1.0 / math.sqrt(window_len)
    table = jnp.concatenate(
        [jnp.cos(phase_angle) * norm_factor, -jnp.sin(phase_angle) * norm_factor], axis=1
    )
    table_high = table.astype(jnp.bfloat16)
    table_low = (table - table_high.astype(jnp.float32)).astype(jnp.bfloat16)
    result = jnp.dot(samples, table_high, preferred_element_type=jnp.float32)
    result = result + jnp.dot(samples, table_low, preferred_element_type=jnp.float32)
    real_part = result[:, :bin_count]
    imag_part = result[:, bin_count:]
    return jnp.stack([real_part, imag_part], axis=1).astype(jnp.bfloat16)


def route_rows(spectra, owners, targets, places, owner_count, empty_id):
    row_count = owners.shape[0]
    owner_hit = owners[:, None] == lax.broadcasted_iota(jnp.int32, (1, owner_count), 1)
    earlier = lax.broadcasted_iota(jnp.int32, (row_count, row_count), 0) > lax.broadcasted_iota(
        jnp.int32, (row_count, row_count), 1
    )
    before = jnp.dot(
        earlier.astype(jnp.bfloat16),
        owner_hit.astype(jnp.bfloat16),
        preferred_element_type=jnp.float32,
    )
    slot_rank = jnp.sum(jnp.where(owner_hit, before, 0.0), axis=1).astype(jnp.int32)
    position = owners * places + slot_rank
    slot_total = owner_count * places
    slot_hit = position[:, None] == lax.broadcasted_iota(jnp.int32, (1, slot_total), 1)
    flat_spectra = spectra.reshape(row_count, -1)
    buffer = lax.dot_general(
        slot_hit.astype(jnp.bfloat16),
        flat_spectra,
        (((0,), (0,)), ((), ())),
        preferred_element_type=jnp.float32,
    )
    buffer = buffer.astype(spectra.dtype)
    labels = jnp.max(jnp.where(slot_hit, targets[:, None], -1), axis=0)
    labels = jnp.where(labels < 0, empty_id, labels)
    return (
        buffer.reshape((owner_count, places) + spectra.shape[1:]),
        labels.reshape(owner_count, places),
    )


def bin_panel(received, labels, shot_rows, point_count):
    freq_count = received.shape[-1]
    flat_rows = received.reshape(-1, 2 * freq_count)
    flat_labels = labels.reshape(-1)
    point_iota = lax.broadcasted_iota(jnp.int32, (1, point_count), 1)

    def one_shot(shot_id):
        local_label = flat_labels - shot_id * point_count
        point_hit = local_label[:, None] == point_iota
        totals = lax.dot_general(
            point_hit.astype(jnp.bfloat16),
            flat_rows,
            (((0,), (0,)), ((), ())),
            preferred_element_type=jnp.float32,
        )
        coverage = jnp.sum(point_hit.astype(jnp.float32), axis=0)
        return (totals / jnp.maximum(coverage, 1.0)[:, None]).astype(jnp.bfloat16)

    panel = lax.map(one_shot, jnp.arange(shot_rows, dtype=jnp.int32))
    return panel.reshape(shot_rows, point_count, 2, freq_count).transpose(3, 2, 0, 1)


def product(left_edge, right_edge):
    return jnp.einsum("bhv,bvy->bhy", left_edge, right_edge, preferred_element_type=jnp.float32)


def local(traces, trace_block, trace_shot, trace_point, recv_panel):
    shot_count = lax.axis_size("shot")
    rcv_count = lax.axis_size("rcv")
    freq_count = recv_panel.shape[0]
    half_points = recv_panel.shape[2] * shot_count
    window_len = traces.shape[2]
    row_count = traces.shape[1]
    part_rows = row_count // rcv_count
    capacity = 2 * part_rows // shot_count
    empty_id = SHOTS_PER_INDEX * half_points
    samples = traces[0]
    owners = trace_block[0, :, 0]
    targets = trace_shot[0] * half_points + trace_point[0]
    spectra = transform_rows(samples, window_len, freq_count)
    buffer, labels = route_rows(
        spectra, owners, targets, rcv_count * capacity, shot_count, empty_id
    )
    received, got_labels = (
        lax.all_to_all(buffer, "shot", split_axis=0, concat_axis=0, tiled=True),
        lax.all_to_all(labels, "shot", split_axis=0, concat_axis=0, tiled=True),
    )
    panel = bin_panel(received, got_labels, SHOTS_PER_INDEX, half_points)
    receiver = lax.all_gather(recv_panel, "shot", axis=2, tiled=True)
    real_part = product(panel[:, 0], receiver[:, 0]) - product(panel[:, 1], receiver[:, 1])
    imag_part = product(panel[:, 0], receiver[:, 1]) + product(panel[:, 1], receiver[:, 0])
    partial_value = jnp.stack([real_part, imag_part], axis=1)
    half_term = lax.optimization_barrier(partial_value.astype(jnp.bfloat16)).astype(jnp.float32)
    result = summed_on_arrival(half_term.astype(jnp.bfloat16), "surf", 2)
    return result.astype(jnp.bfloat16)


def solution(mesh):
    in_specs = (
        P("surf", "shot", None),
        P("surf", "shot", None),
        P("surf", "shot"),
        P("surf", "shot"),
        P(None, None, ("shot", "surf"), "rcv"),
    )
    out_specs = P(None, None, ("shot", "surf"), "rcv")
    return jax.shard_map(local, mesh=mesh, in_specs=in_specs, out_specs=out_specs, check_vma=False)
```

profile of v0, /device:TPU:23, one launch (start us, length us, event | category | flops | bytes accessed | tf_op | source)
XLA Modules:
  0.0 263.6 jit_solution(1235971979130966523)
XLA Ops:
  15.5 9.4 %all-to-all-start.1 = ((bf16[16,128,2,129]{1,2,3,0:T(2,128)(2,1)}), bf16[16,128,2,129]{1,2,3,0:T(2,128)(2,1)S(1)}, u32[]{:S(2)}, u32[]{:S(2)}) async-start(bf16[16,128,2,129]{1,2,3,0:T(2,128)(2,1)} %copy.36), calls=%async_computation.1 | async-start | bytes 2113536 | tf_op jit(solution)/shard_map/all_to_all | solution.py:115
  27.2 33.8 %all-to-all-done.1 = bf16[16,128,2,129]{1,2,3,0:T(2,128)(2,1)S(1)} async-done(((bf16[16,128,2,129]{1,2,3,0:T(2,128)(2,1)}), bf16[16,128,2,129]{1,2,3,0:T(2,128)(2,1)S(1)}, u32[]{:S(2)}, u32[]{:S(2)}) %all-to-all-start.1) | async-done | bytes 1056800 | tf_op jit(solution)/shard_map/all_to_all | solution.py:115
  61.0 5.1 %all-to-all-start = ((s32[16,1,128]{2,1,0:T(1,128)}), s32[16,1,128]{2,1,0:T(1,128)S(1)}, u32[]{:S(2)}, u32[]{:S(2)}) async-start(s32[16,1,128]{2,1,0:T(1,128)} %compare_select_fusion), calls=%async_computation | async-start | bytes 16384 | tf_op jit(solution)/shard_map/all_to_all | solution.py:116
  66.1 8.1 %copy.44 = bf16[16,128,2,129]{3,2,1,0:T(2,128)(2,1)S(1)} copy(bf16[16,128,2,129]{1,2,3,0:T(2,128)(2,1)} %copy-done.2) | data formatting | bytes 2113536
  76.2 74.6 %while.11 = (s32[]{:T(128)}, bf16[16,256,258]{1,2,0:T(8,128)(2,1)}, s32[16]{0:T(128)S(1)}, s32[2048]{0:T(1024)S(1)}, bf16[2048,258]{1,0:T(8,128)(2,1)}, /*index=5*/s32[]{:T(128)}, s32[1]{0:T(128)}) while((s32[]{:T(128)}, bf16[16,256,258]{1,2,0:T(8,128)(2,1)}, s32[16]{0:T(128)S(1)}, s32[2048]{0:T(1024)S(1)}, ...), condition=%wide.region_4.5_spmd.clone, body=%wide.region_2.4_spmd.clone.sunk | while | flops 272763904 | bytes 1745513 | solution.py:89
  77.8 3.1 %fusion.50 = bf16[16,256,258]{1,2,0:T(8,128)(2,1)} fusion(bf16[16,256,258]{1,2,0:T(8,128)(2,1)} %get-tuple-element.128, s32[]{:T(128)} %get-tuple-element.127, bf16[2048,258]{1,0:T(8,128)(2,1)} %get-tuple-element.138, s32[2048]{0:T(1024)S(1)} %broadcast_subtract_fusion.2, f32[256]{0:T(256)S(1)} %broadcast_maximum_fusion.2), kind=kOutput, calls=%fused_computation.8.clone.1 | convolution fusion | flops 271188992 | bytes 1717760 | tf_op jit(solution)/shard_map/while/body/eval_jaxpr/dot_general | solution.py:80
  82.5 3.0 %fusion.50 = bf16[16,256,258]{1,2,0:T(8,128)(2,1)} fusion(bf16[16,256,258]{1,2,0:T(8,128)(2,1)} %get-tuple-element.128, s32[]{:T(128)} %get-tuple-element.127, bf16[2048,258]{1,0:T(8,128)(2,1)} %get-tuple-element.138, s32[2048]{0:T(1024)S(1)} %broadcast_subtract_fusion.2, f32[256]{0:T(256)S(1)} %broadcast_maximum_fusion.2), kind=kOutput, calls=%fused_computation.8.clone.1 | convolution fusion | flops 271188992 | bytes 1717760 | tf_op jit(solution)/shard_map/while/body/eval_jaxpr/dot_general | solution.py:80
  87.2 3.1 %fusion.50 = bf16[16,256,258]{1,2,0:T(8,128)(2,1)} fusion(bf16[16,256,258]{1,2,0:T(8,128)(2,1)} %get-tuple-element.128, s32[]{:T(128)} %get-tuple-element.127, bf16[2048,258]{1,0:T(8,128)(2,1)} %get-tuple-element.138, s32[2048]{0:T(1024)S(1)} %broadcast_subtract_fusion.2, f32[256]{0:T(256)S(1)} %broadcast_maximum_fusion.2), kind=kOutput, calls=%fused_computation.8.clone.1 | convolution fusion | flops 271188992 | bytes 1717760 | tf_op jit(solution)/shard_map/while/body/eval_jaxpr/dot_general | solution.py:80
  96.5 3.1 %fusion.50 = bf16[16,256,258]{1,2,0:T(8,128)(2,1)} fusion(bf16[16,256,258]{1,2,0:T(8,128)(2,1)} %get-tuple-element.128, s32[]{:T(128)} %get-tuple-element.127, bf16[2048,258]{1,0:T(8,128)(2,1)} %get-tuple-element.138, s32[2048]{0:T(1024)S(1)} %broadcast_subtract_fusion.2, f32[256]{0:T(256)S(1)} %broadcast_maximum_fusion.2), kind=kOutput, calls=%fused_computation.8.clone.1 | convolution fusion | flops 271188992 | bytes 1717760 | tf_op jit(solution)/shard_map/while/body/eval_jaxpr/dot_general | solution.py:80
  101.1 3.0 %fusion.50 = bf16[16,256,258]{1,2,0:T(8,128)(2,1)} fusion(bf16[16,256,258]{1,2,0:T(8,128)(2,1)} %get-tuple-element.128, s32[]{:T(128)} %get-tuple-element.127, bf16[2048,258]{1,0:T(8,128)(2,1)} %get-tuple-element.138, s32[2048]{0:T(1024)S(1)} %broadcast_subtract_fusion.2, f32[256]{0:T(256)S(1)} %broadcast_maximum_fusion.2), kind=kOutput, calls=%fused_computation.8.clone.1 | convolution fusion | flops 271188992 | bytes 1717760 | tf_op jit(solution)/shard_map/while/body/eval_jaxpr/dot_general | solution.py:80
  105.8 3.0 %fusion.50 = bf16[16,256,258]{1,2,0:T(8,128)(2,1)} fusion(bf16[16,256,258]{1,2,0:T(8,128)(2,1)} %get-tuple-element.128, s32[]{:T(128)} %get-tuple-element.127, bf16[2048,258]{1,0:T(8,128)(2,1)} %get-tuple-element.138, s32[2048]{0:T(1024)S(1)} %broadcast_subtract_fusion.2, f32[256]{0:T(256)S(1)} %broadcast_maximum_fusion.2), kind=kOutput, calls=%fused_computation.8.clone.1 | convolution fusion | flops 271188992 | bytes 1717760 | tf_op jit(solution)/shard_map/while/body/eval_jaxpr/dot_general | solution.py:80
  110.5 3.1 %fusion.50 = bf16[16,256,258]{1,2,0:T(8,128)(2,1)} fusion(bf16[16,256,258]{1,2,0:T(8,128)(2,1)} %get-tuple-element.128, s32[]{:T(128)} %get-tuple-element.127, bf16[2048,258]{1,0:T(8,128)(2,1)} %get-tuple-element.138, s32[2048]{0:T(1024)S(1)} %broadcast_subtract_fusion.2, f32[256]{0:T(256)S(1)} %broadcast_maximum_fusion.2), kind=kOutput, calls=%fused_computation.8.clone.1 | convolution fusion | flops 271188992 | bytes 1717760 | tf_op jit(solution)/shard_map/while/body/eval_jaxpr/dot_general | solution.py:80
  115.1 3.0 %fusion.50 = bf16[16,256,258]{1,2,0:T(8,128)(2,1)} fusion(bf16[16,256,258]{1,2,0:T(8,128)(2,1)} %get-tuple-element.128, s32[]{:T(128)} %get-tuple-element.127, bf16[2048,258]{1,0:T(8,128)(2,1)} %get-tuple-element.138, s32[2048]{0:T(1024)S(1)} %broadcast_subtract_fusion.2, f32[256]{0:T(256)S(1)} %broadcast_maximum_fusion.2), kind=kOutput, calls=%fused_computation.8.clone.1 | convolution fusion | flops 271188992 | bytes 1717760 | tf_op jit(solution)/shard_map/while/body/eval_jaxpr/dot_general | solution.py:80
  119.8 3.1 %fusion.50 = bf16[16,256,258]{1,2,0:T(8,128)(2,1)} fusion(bf16[16,256,258]{1,2,0:T(8,128)(2,1)} %get-tuple-element.128, s32[]{:T(128)} %get-tuple-element.127, bf16[2048,258]{1,0:T(8,128)(2,1)} %get-tuple-element.138, s32[2048]{0:T(1024)S(1)} %broadcast_subtract_fusion.2, f32[256]{0:T(256)S(1)} %broadcast_maximum_fusion.2), kind=kOutput, calls=%fused_computation.8.clone.1 | convolution fusion | flops 271188992 | bytes 1717760 | tf_op jit(solution)/shard_map/while/body/eval_jaxpr/dot_general | solution.py:80
  124.5 3.0 %fusion.50 = bf16[16,256,258]{1,2,0:T(8,128)(2,1)} fusion(bf16[16,256,258]{1,2,0:T(8,128)(2,1)} %get-tuple-element.128, s32[]{:T(128)} %get-tuple-element.127, bf16[2048,258]{1,0:T(8,128)(2,1)} %get-tuple-element.138, s32[2048]{0:T(1024)S(1)} %broadcast_subtract_fusion.2, f32[256]{0:T(256)S(1)} %broadcast_maximum_fusion.2), kind=kOutput, calls=%fused_computation.8.clone.1 | convolution fusion | flops 271188992 | bytes 1717760 | tf_op jit(solution)/shard_map/while/body/eval_jaxpr/dot_general | solution.py:80
  129.1 3.1 %fusion.50 = bf16[16,256,258]{1,2,0:T(8,128)(2,1)} fusion(bf16[16,256,258]{1,2,0:T(8,128)(2,1)} %get-tuple-element.128, s32[]{:T(128)} %get-tuple-element.127, bf16[2048,258]{1,0:T(8,128)(2,1)} %get-tuple-element.138, s32[2048]{0:T(1024)S(1)} %broadcast_subtract_fusion.2, f32[256]{0:T(256)S(1)} %broadcast_maximum_fusion.2), kind=kOutput, calls=%fused_computation.8.clone.1 | convolution fusion | flops 271188992 | bytes 1717760 | tf_op jit(solution)/shard_map/while/body/eval_jaxpr/dot_general | solution.py:80
  133.8 3.0 %fusion.50 = bf16[16,256,258]{1,2,0:T(8,128)(2,1)} fusion(bf16[16,256,258]{1,2,0:T(8,128)(2,1)} %get-tuple-element.128, s32[]{:T(128)} %get-tuple-element.127, bf16[2048,258]{1,0:T(8,128)(2,1)} %get-tuple-element.138, s32[2048]{0:T(1024)S(1)} %broadcast_subtract_fusion.2, f32[256]{0:T(256)S(1)} %broadcast_maximum_fusion.2), kind=kOutput, calls=%fused_computation.8.clone.1 | convolution fusion | flops 271188992 | bytes 1717760 | tf_op jit(solution)/shard_map/while/body/eval_jaxpr/dot_general | solution.py:80
  138.4 3.0 %fusion.50 = bf16[16,256,258]{1,2,0:T(8,128)(2,1)} fusion(bf16[16,256,258]{1,2,0:T(8,128)(2,1)} %get-tuple-element.128, s32[]{:T(128)} %get-tuple-element.127, bf16[2048,258]{1,0:T(8,128)(2,1)} %get-tuple-element.138, s32[2048]{0:T(1024)S(1)} %broadcast_subtract_fusion.2, f32[256]{0:T(256)S(1)} %broadcast_maximum_fusion.2), kind=kOutput, calls=%fused_computation.8.clone.1 | convolution fusion | flops 271188992 | bytes 1717760 | tf_op jit(solution)/shard_map/while/body/eval_jaxpr/dot_general | solution.py:80
  143.1 3.1 %fusion.50 = bf16[16,256,258]{1,2,0:T(8,128)(2,1)} fusion(bf16[16,256,258]{1,2,0:T(8,128)(2,1)} %get-tuple-element.128, s32[]{:T(128)} %get-tuple-element.127, bf16[2048,258]{1,0:T(8,128)(2,1)} %get-tuple-element.138, s32[2048]{0:T(1024)S(1)} %broadcast_subtract_fusion.2, f32[256]{0:T(256)S(1)} %broadcast_maximum_fusion.2), kind=kOutput, calls=%fused_computation.8.clone.1 | convolution fusion | flops 271188992 | bytes 1717760 | tf_op jit(solution)/shard_map/while/body/eval_jaxpr/dot_general | solution.py:80
  147.7 3.1 %fusion.50 = bf16[16,256,258]{1,2,0:T(8,128)(2,1)} fusion(bf16[16,256,258]{1,2,0:T(8,128)(2,1)} %get-tuple-element.128, s32[]{:T(128)} %get-tuple-element.127, bf16[2048,258]{1,0:T(8,128)(2,1)} %get-tuple-element.138, s32[2048]{0:T(1024)S(1)} %broadcast_subtract_fusion.2, f32[256]{0:T(256)S(1)} %broadcast_maximum_fusion.2), kind=kOutput, calls=%fused_computation.8.clone.1 | convolution fusion | flops 271188992 | bytes 1717760 | tf_op jit(solution)/shard_map/while/body/eval_jaxpr/dot_general | solution.py:80
  152.9 73.6 %all-gather.2.cloned.1.call-done = bf16[129,2,256,128]{3,2,0,1:T(8,128)(2,1)} async-done(((bf16[129,2,16,128]{3,2,0,1:T(8,128)(2,1)}), bf16[129,2,256,128]{3,2,0,1:T(8,128)(2,1)}) %all-gather.2.cloned.1.call-update) | async-done | bytes 16908304 | tf_op jit(solution)/shard_map/all_gather | solution.py:119
  226.4 4.8 %fusion.12 = f32[129,16,128]{2,1,0:T(8,128)S(1)} fusion(bf16[129,2,256,128]{3,2,0,1:T(8,128)(2,1)} %all-gather.2.cloned.1.call-done, bf16[129,2,16,256]{3,2,0,1:T(8,128)(2,1)S(1)} %bitcast.76), kind=kOutput, calls=%fused_computation.18 | convolution fusion | flops 135266304 | bytes 10567680 | tf_op jit(solution)/shard_map/bhv,bvy->bhy/dot_general | solution.py:94
  231.2 5.4 %fusion.11 = f32[129,16,128]{2,1,0:T(8,128)S(1)} fusion(bf16[129,2,256,128]{3,2,0,1:T(8,128)(2,1)} %all-gather.2.cloned.1.call-done, bf16[129,2,16,256]{3,2,0,1:T(8,128)(2,1)S(1)} %bitcast.77), kind=kOutput, calls=%fused_computation.17 | convolution fusion | flops 135266304 | bytes 10567680 | tf_op jit(solution)/shard_map/bhv,bvy->bhy/dot_general | solution.py:94
  240.0 15.4 %all_to_all.16 = bf16[2,129,2,8,128]{4,3,1,2,0:T(8,128)(2,1)S(1)} all-to-all(bf16[2,129,2,8,128]{4,3,1,2,0:T(8,128)(2,1)S(1)} %copy_bitcast_fusion), channel_id=1, replica_groups=mesh['shot'=16,'rcv'=8,'surf'=2] {'surf'}, dimensions={0} | all-to-all | bytes 2113536 | tf_op jit(solution)/shard_map/all_to_all | solution.py:17
  (106 shorter events, 38.1 us)
Async XLA Ops:
  6.5 3.0 %copy-start = (bf16[1,1024,256]{2,1,0:T(8,128)(2,1)S(1)}, bf16[1,1024,256]{2,1,0:T(8,128)(2,1)}, u32[]{:S(2)}) copy-start(bf16[1,1024,256]{2,1,0:T(8,128)(2,1)} %param.7) | copy-start | bytes 1572868
  6.5 219.9 %all-gather.2.cloned.1.call-start = ((), (), s32[]{:S(2)}) async-start(), calls=%async_computation.3 | async-start | bytes 17965056 | tf_op jit(solution)/shard_map/all_gather | solution.py:119
  10.3 0.7 copy-start.3
  13.7 11.2 %copy-start.4 = (s32[1,1024]{1,0:T(1,128)S(1)}, s32[1,1024]{1,0:T(1,128)}, u32[]{:S(2)}) copy-start(s32[1,1024]{1,0:T(1,128)} %param.10) | copy-start | bytes 12292
  13.7 11.2 %copy-start.5 = (s32[1,1024]{1,0:T(1,128)S(1)}, s32[1,1024]{1,0:T(1,128)}, u32[]{:S(2)}) copy-start(s32[1,1024]{1,0:T(1,128)} %param.9) | copy-start | bytes 12292
  15.5 45.4 %all-to-all-start.1 = ((bf16[16,128,2,129]{1,2,3,0:T(2,128)(2,1)}), bf16[16,128,2,129]{1,2,3,0:T(2,128)(2,1)S(1)}, u32[]{:S(2)}, u32[]{:S(2)}) async-start(bf16[16,128,2,129]{1,2,3,0:T(2,128)(2,1)} %copy.36), calls=%async_computation.1 | async-start | bytes 2113536 | tf_op jit(solution)/shard_map/all_to_all | solution.py:115
  61.0 5.1 %copy-start.2 = (bf16[16,128,2,129]{1,2,3,0:T(2,128)(2,1)}, bf16[16,128,2,129]{1,2,3,0:T(2,128)(2,1)S(1)}, u32[]{:S(2)}) copy-start(bf16[16,128,2,129]{1,2,3,0:T(2,128)(2,1)S(1)} %all-to-all-done.1) | copy-start | bytes 3170308
  61.0 15.3 %all-to-all-start = ((s32[16,1,128]{2,1,0:T(1,128)}), s32[16,1,128]{2,1,0:T(1,128)S(1)}, u32[]{:S(2)}, u32[]{:S(2)}) async-start(s32[16,1,128]{2,1,0:T(1,128)} %compare_select_fusion), calls=%async_computation | async-start | bytes 16384 | tf_op jit(solution)/shard_map/all_to_all | solution.py:116
  226.4 10.6 %copy-start.1 = (bf16[129,2,256,128]{3,2,0,1:T(8,128)(2,1)S(1)}, bf16[129,2,256,128]{3,2,0,1:T(8,128)(2,1)}, u32[]{:S(2)}) copy-start(bf16[129,2,256,128]{3,2,0,1:T(8,128)(2,1)} %all-gather.2.cloned.1.call-done) | copy-start | bytes 50724868
Sparse Core Ops, SparseCore 0:
  9.1 217.2 all-gather.1
where the time goes:
time: 265 us; the launch traced here: 264 us
  waiting for transfers between devices  107 us (40%)
  matrix products  64.6 us (24%)
  local copies, waits for them, and re-layouts  28.3 us (11%)
  blocking collectives  15.4 us (6%)
  starting transfers between devices  14.5 us (5%)
  between operations  13.6 us (5%)
  loops' own time  10.6 us (4%)
  other arithmetic  9.28 us (4%)
    all_gather x1, waiting for transfers between devices, local(): receiver = lax.all_gather(recv_panel, 'shot', axis=2, tiled=True)  73.6 us
    dot_general x16, matrix products, one_shot(): lax.dot_general(point_hit.astype(jnp.bfloat16), flat_rows, (((0,), (0,)),...  48.9 us
    all_to_all x1, waiting for transfers between devices, local(): lax.all_to_all(buffer, 'shot', split_axis=0, concat_axis=0, tiled=True)  33.8 us
    all_to_all x1, blocking collectives, summed_on_arrival(): parts = lax.all_to_all(split_up(array, dim, size), axis, 0, 0, tiled=True)  15.4 us
    unnamed x17, local copies, waits for them, and re-layouts  13.8 us
    dot_general x4, matrix products, product(): jnp.einsum('bhv,bvy->bhy', left_edge, right_edge, preferred_element_type=...  12.7 us
    another operation x1, loops' own time, bin_panel(): panel = lax.map(one_shot, jnp.arange(shot_rows, dtype=jnp.int32))  10.6 us
    all_to_all x1, starting transfers between devices, local(): lax.all_to_all(buffer, 'shot', split_axis=0, concat_axis=0, tiled=True)  9.39 us
  transfers between devices with their start and end apart: 3, of which 2 were waited for; matrix products, arithmetic and copies ran while one was open for 32% of the time, Pallas kernels for 0%

commit v1 on v0

--- a/solution.py
+++ b/solution.py
@@ -116,7 +116,9 @@
         lax.all_to_all(labels, "shot", split_axis=0, concat_axis=0, tiled=True),
     )
     panel = bin_panel(received, got_labels, SHOTS_PER_INDEX, half_points)
-    receiver = lax.all_gather(recv_panel, "shot", axis=2, tiled=True)
+    receiver = jnp.concatenate(
+        lax.all_to_all(jnp.stack([recv_panel] * lax.axis_size("shot")), "shot", 0, 0), axis=2
+    )
     real_part = product(panel[:, 0], receiver[:, 0]) - product(panel[:, 1], receiver[:, 1])
     imag_part = product(panel[:, 0], receiver[:, 1]) + product(panel[:, 1], receiver[:, 0])
     partial_value = jnp.stack([real_part, imag_part], axis=1)

time: 265 us -> 472 us (1.78)
  the two profiles are of different devices: /device:TPU:23 before, /device:TPU:143 now
where the time goes in v1:
time: 472 us; the launch traced here: 470 us
  waiting for transfers between devices  320 us (68%)
  matrix products  57.4 us (12%)
  local copies, waits for them, and re-layouts  43.5 us (9%)
  starting transfers between devices  24 us (5%)
  other arithmetic  10.7 us (2%)
  loops' own time  10.2 us (2%)
  blocking collectives  4.72 us (1%)
    all_to_all x1, waiting for transfers between devices, local(): lax.all_to_all(jnp.stack([recv_panel] * lax.axis_size('shot')), 'shot', 0...  298 us
    dot_general x16, matrix products, one_shot(): lax.dot_general(point_hit.astype(jnp.bfloat16), flat_rows, (((0,), (0,)),...  48.6 us
    all_to_all x1, waiting for transfers between devices, local(): lax.all_to_all(buffer, 'shot', split_axis=0, concat_axis=0, tiled=True)  21.6 us
    unnamed x11, local copies, waits for them, and re-layouts  12 us
    another operation x1, loops' own time, bin_panel(): panel = lax.map(one_shot, jnp.arange(shot_rows, dtype=jnp.int32))  10.2 us
    dynamic_slice x16, local copies, waits for them, and re-layouts, bin_panel(): panel = lax.map(one_shot, jnp.arange(shot_rows, dtype=jnp.int32))  10.2 us
    reshape x1, local copies, waits for them, and re-layouts, local(): jnp.concatenate(lax.all_to_all(jnp.stack([recv_panel] * lax.axis_size('sh...  10 us
  transfers between devices with their start and end apart: 3, of which 2 were waited for; matrix products, arithmetic and copies ran while one was open for 18% of the time, Pallas kernels for 0%

profile of v1, /device:TPU:143, one launch (start us, length us, event | category | flops | bytes accessed | tf_op | source)
XLA Modules:
  0.0 470.4 jit_solution(15858669965410426840)
XLA Ops:
  4.9 7.6 %all-to-all-start = ((s32[16,1,128]{2,1,0:T(1,128)}), s32[16,1,128]{2,1,0:T(1,128)S(1)}, u32[]{:S(2)}, u32[]{:S(2)}) async-start(s32[16,1,128]{2,1,0:T(1,128)} %compare_select_fusion), calls=%async_computation | async-start | bytes 16384 | tf_op jit(solution)/shard_map/all_to_all | solution.py:116
  18.1 7.6 %all-to-all-start.1 = ((bf16[16,128,2,129]{1,2,3,0:T(2,128)(2,1)}), bf16[16,128,2,129]{1,2,3,0:T(2,128)(2,1)S(1)}, u32[]{:S(2)}, u32[]{:S(2)}) async-start(bf16[16,128,2,129]{1,2,3,0:T(2,128)(2,1)} %copy.39), calls=%async_computation.1 | async-start | bytes 2113536 | tf_op jit(solution)/shard_map/all_to_all | solution.py:115
  27.1 21.6 %all-to-all-done.1 = bf16[16,128,2,129]{1,2,3,0:T(2,128)(2,1)S(1)} async-done(((bf16[16,128,2,129]{1,2,3,0:T(2,128)(2,1)}), bf16[16,128,2,129]{1,2,3,0:T(2,128)(2,1)S(1)}, u32[]{:S(2)}, u32[]{:S(2)}) %all-to-all-start.1) | async-done | bytes 1056800 | tf_op jit(solution)/shard_map/all_to_all | solution.py:115
  48.7 6.2 %stack.46 = bf16[16,129,2,16,128]{4,3,1,2,0:T(8,128)(2,1)} broadcast(bf16[129,2,16,128]{3,2,0,1:T(8,128)(2,1)S(1)} %copy.43), dimensions={1,2,3,4} | broadcast | bytes 17965056 | tf_op jit(solution)/shard_map/stack | solution.py:120
  54.9 8.8 %all-to-all-start.2 = ((bf16[16,129,2,16,128]{4,3,1,2,0:T(8,128)(2,1)}), bf16[16,129,2,16,128]{4,3,1,2,0:T(8,128)(2,1)}, u32[]{:S(2)}, u32[]{:S(2)}) async-start(bf16[16,129,2,16,128]{4,3,1,2,0:T(8,128)(2,1)} %stack.46), calls=%async_computation.2 | async-start | bytes 33816576 | tf_op jit(solution)/shard_map/all_to_all | solution.py:120
  63.7 8.1 %copy.48 = bf16[16,128,2,129]{3,2,1,0:T(2,128)(2,1)S(1)} copy(bf16[16,128,2,129]{1,2,3,0:T(2,128)(2,1)} %copy-done.2) | data formatting | bytes 2113536
  73.9 74.7 %while.11 = (s32[]{:T(128)}, bf16[16,256,258]{1,2,0:T(8,128)(2,1)}, s32[16]{0:T(128)S(1)}, s32[2048]{0:T(1024)S(1)}, bf16[2048,258]{1,0:T(8,128)(2,1)}, /*index=5*/s32[]{:T(128)}, s32[1]{0:T(128)}) while((s32[]{:T(128)}, bf16[16,256,258]{1,2,0:T(8,128)(2,1)}, s32[16]{0:T(128)S(1)}, s32[2048]{0:T(1024)S(1)}, ...), condition=%wide.region_4.5_spmd.clone, body=%wide.region_2.4_spmd.clone.sunk | while | flops 272763904 | bytes 1745013 | solution.py:89
  75.5 3.0 fusion.50
  84.8 3.0 fusion.50
  94.2 3.1 fusion.50
  98.9 3.0 fusion.50
  103.5 3.0 fusion.50
  108.2 3.0 fusion.50
  112.9 3.1 fusion.50
  117.6 3.0 fusion.50
  122.2 3.0 fusion.50
  126.9 3.0 fusion.50
  131.6 3.0 fusion.50
  136.2 3.0 fusion.50
  140.9 3.0 fusion.50
  145.6 3.0 fusion.50
  150.6 298.2 %all-to-all-done.2 = bf16[16,129,2,16,128]{4,3,1,2,0:T(8,128)(2,1)} async-done(((bf16[16,129,2,16,128]{4,3,1,2,0:T(8,128)(2,1)}), bf16[16,129,2,16,128]{4,3,1,2,0:T(8,128)(2,1)}, u32[]{:S(2)}, u32[]{:S(2)}) %all-to-all-start.2) | async-done | bytes 16908320 | tf_op jit(solution)/shard_map/all_to_all | solution.py:120
  448.8 10.0 %copy.44 = bf16[129,2,16,16,128]{4,3,2,0,1:T(8,128)(2,1)S(1)} copy(bf16[129,2,16,16,128]{4,3,0,1,2:T(8,128)(2,1)} %bitcast.11) | data formatting | bytes 33816576 | tf_op jit(solution)/shard_map/reshape | solution.py:119
  464.3 4.7 %all_to_all.21 = bf16[2,129,2,8,128]{4,3,1,2,0:T(8,128)(2,1)S(1)} all-to-all(bf16[2,129,2,8,128]{4,3,1,2,0:T(8,128)(2,1)S(1)} %copy_bitcast_fusion), channel_id=1, replica_groups=mesh['shot'=16,'rcv'=8,'surf'=2] {'surf'}, dimensions={0} | all-to-all | bytes 2113536 | tf_op jit(solution)/shard_map/all_to_all | solution.py:17
  (101 shorter events, 44.7 us)
Async XLA Ops:
  0.0 13.1 %copy-start = (bf16[1,1024,256]{2,1,0:T(8,128)(2,1)S(1)}, bf16[1,1024,256]{2,1,0:T(8,128)(2,1)}, u32[]{:S(2)}) copy-start(bf16[1,1024,256]{2,1,0:T(8,128)(2,1)} %param.7) | copy-start | bytes 1572868
  4.9 13.2 %all-to-all-start = ((s32[16,1,128]{2,1,0:T(1,128)}), s32[16,1,128]{2,1,0:T(1,128)S(1)}, u32[]{:S(2)}, u32[]{:S(2)}) async-start(s32[16,1,128]{2,1,0:T(1,128)} %compare_select_fusion), calls=%async_computation | async-start | bytes 16384 | tf_op jit(solution)/shard_map/all_to_all | solution.py:116
  18.1 30.6 %all-to-all-start.1 = ((bf16[16,128,2,129]{1,2,3,0:T(2,128)(2,1)}), bf16[16,128,2,129]{1,2,3,0:T(2,128)(2,1)S(1)}, u32[]{:S(2)}, u32[]{:S(2)}) async-start(bf16[16,128,2,129]{1,2,3,0:T(2,128)(2,1)} %copy.39), calls=%async_computation.1 | async-start | bytes 2113536 | tf_op jit(solution)/shard_map/all_to_all | solution.py:115
  48.7 6.2 %copy-start.2 = (bf16[16,128,2,129]{1,2,3,0:T(2,128)(2,1)}, bf16[16,128,2,129]{1,2,3,0:T(2,128)(2,1)S(1)}, u32[]{:S(2)}) copy-start(bf16[16,128,2,129]{1,2,3,0:T(2,128)(2,1)S(1)} %all-to-all-done.1) | copy-start | bytes 3170308
  54.9 393.9 %all-to-all-start.2 = ((bf16[16,129,2,16,128]{4,3,1,2,0:T(8,128)(2,1)}), bf16[16,129,2,16,128]{4,3,1,2,0:T(8,128)(2,1)}, u32[]{:S(2)}, u32[]{:S(2)}) async-start(bf16[16,129,2,16,128]{4,3,1,2,0:T(8,128)(2,1)} %stack.46), calls=%async_computation.2 | async-start | bytes 33816576 | tf_op jit(solution)/shard_map/all_to_all | solution.py:120
  464.1 6.3 %copy-start.1 = (bf16[1,1024,256]{2,1,0:T(8,128)(2,1)S(1)}, bf16[1,1024,256]{2,1,0:T(8,128)(2,1)}, u32[]{:S(2)}) copy-start(bf16[1,1024,256]{2,1,0:T(8,128)(2,1)} %param.7) | copy-start | bytes 1572868
